TPU v7x, 32 devices: a whole 2x2x4 slice. The times are simulated.
32 devices in a mesh: grp: 2 (over y), seq: 4 (over z), tp: 2 (over x), pr: 2 (over core).
Axes of the slice: x: 2, y: 2, z: 4, core: 2. Of those that a mesh axis runs over, the one named last changes fastest.
Arguments:
- dna_feats: bfloat16 [2048, 768], P(('grp', 'seq', 'pr'), 'tp'), parts along dimension 0, may hold values from -6 to 6
- conv_w: bfloat16 [5, 768, 1536], P(None, 'pr', 'tp'), may hold values from -0.09375 to 0.09375
- conv_gain: float32 [1536], P('tp'), may hold values from 0.1 to 1.9
- attn_gain: float32 [1536], replicated, may hold values from 0.1 to 1.9
- wq: bfloat16 [1536, 1024], P('pr', 'tp'), as said below
- wk: bfloat16 [1536, 1024], P('pr', 'tp'), as said below
- wv: bfloat16 [1536, 1536], P('pr', 'tp'), may hold values from -0.3125 to 0.3125
- wo: bfloat16 [1536, 1536], P('tp', 'pr'), may hold values from -0.15625 to 0.15625
- pair_w: bfloat16 [1536, 256], P('tp'), may hold values from -0.3125 to 0.3125
- pair_in: bfloat16 [128, 64, 128], P(('grp', 'seq', 'tp'), 'pr'), parts along dimension 0, may hold values from -6 to 6
- pair_gain: float32 [128], replicated, may hold values from 0.1 to 1.9
- pair_w1: bfloat16 [128, 256], replicated, may hold values from -0.5 to 0.5
- pair_w2: bfloat16 [256, 128], replicated, may hold values from -0.375 to 0.375
Outputs:
- trunk: bfloat16 [2048, 1536], P(('grp', 'seq', 'pr'), 'tp'), parts along dimension 0
- pair_out: bfloat16 [128, 64, 128], P(('grp', 'seq', 'tp'), 'pr'), parts along dimension 0
There are 2 independent parts, one for each index of `grp`. A program takes and returns all parts, laid end to end along the dimension named above; an argument that names none is the same for every part. Nothing has to cross between parts.
Inputs may be any that keep to these rules, and one draw needn't show every extreme that they name: `wq`: before rounding to bfloat16, entries lie between -3.5 / sqrt(1536) and 3.5 / sqrt(1536). `wk`: before rounding to bfloat16, entries lie between -8.75 / sqrt(1536) and 8.75 / sqrt(1536).
All inputs are finite; a program needn't handle non-finite values.
Results may differ from a plain program's by a relative error of at most 0.013.
The roundings to bfloat16 on the way count: a program that leaves them out, or rounds other values in their place, can miss the bound.
Values may be sent and summed in bfloat16 or wider, within the bound.
A program may use at most 64 MiB of HBM per device.

v0:
```python
import math
import jax
import jax.numpy as jnp
from jax import lax
from jax.sharding import PartitionSpec as P

QK = 128
HV = 192
POOL = 16
EPSILON = 1e-06


def extended(value, sides, width):
    for axis, dim in sides:
        devices, length = (lax.axis_size(axis), value.shape[dim])
        up = [(i, (i + 1) % devices) for i in range(devices - 1)]
        down = [(j, i) for i, j in up]
        last = lax.slice_in_dim(value, length - width, length, axis=dim)
        first = lax.slice_in_dim(value, 0, width, axis=dim)
        before = lax.ppermute(last, axis, up)
        after = lax.ppermute(first, axis, down)
        value = jnp.concatenate([before, value, after], axis=dim)
    return value


def rms_scale(values):
    return lax.rsqrt(jnp.mean(values * values, axis=-1, keepdims=True) + EPSILON)


def attention_start(query_block):
    head_count = query_block.shape[1]
    row_count = query_block.shape[0]
    highest = jnp.full((head_count, row_count), -1e30, jnp.float32)
    totals = jnp.zeros((head_count, row_count), jnp.float32)
    mixed = jnp.zeros((row_count, head_count, HV), jnp.float32)
    return (highest, totals, mixed)


def attention_step(query_block, carry, pieces):
    factor = 1.0 / math.sqrt(QK)
    highest, totals, mixed = carry
    key_piece, value_piece = pieces
    scores = (
        jnp.einsum("qhd,khd->hqk", query_block, key_piece, preferred_element_type=jnp.float32)
        * factor
    )
    new_high = jnp.maximum(highest, jnp.max(scores, axis=-1))
    weights = jnp.exp(scores - new_high[:, :, None])
    totals = jnp.sum(weights, axis=-1)
    added = jnp.einsum(
        "hqk,khd->qhd",
        weights.astype(jnp.bfloat16),
        value_piece,
        preferred_element_type=jnp.float32,
    )
    mixed = added
    return (new_high, totals, mixed)


def attention_finish(carry):
    highest, totals, mixed = carry
    return (mixed / jnp.transpose(totals)[:, :, None]).astype(jnp.bfloat16)


def local(
    dna_feats,
    conv_w,
    conv_gain,
    attn_gain,
    wq,
    wk,
    wv,
    wo,
    pair_w,
    pair_in,
    pair_gain,
    pair_w1,
    pair_w2,
):
    row_count = dna_feats.shape[0]
    reach = conv_w.shape[0] // 2
    rimmed = extended(dna_feats, ((("seq", "pr"), 0),), reach)
    channels = lax.all_gather(rimmed, "tp", axis=1, tiled=True)
    conv_empty = jnp.zeros((row_count, conv_w.shape[2]), jnp.float32)
    total = conv_empty
    piece = lax.all_gather(conv_w, "pr", axis=1, tiled=True)
    sliced = channels
    for offset in range(piece.shape[0]):
        total = total + jnp.dot(
            sliced[offset : offset + row_count], piece[offset], preferred_element_type=jnp.float32
        )
    squares = lax.psum(jnp.sum(total * total, axis=1, keepdims=True), "tp")
    model_width = total.shape[1] * lax.axis_size("tp")
    hidden_conv = jax.nn.gelu(
        total * lax.rsqrt(squares / model_width + EPSILON) * conv_gain
    ).astype(jnp.bfloat16)
    trunk_full = lax.all_gather(hidden_conv, "tp", axis=1, tiled=True)
    trunk_wide = trunk_full.astype(jnp.float32)
    normed = (trunk_wide * rms_scale(trunk_wide) * attn_gain).astype(jnp.bfloat16)
    query_width = wq.shape[1]
    pieces = (
        lax.all_gather(wq, "pr", axis=0, tiled=True),
        lax.all_gather(wk, "pr", axis=0, tiled=True),
        lax.all_gather(wv, "pr", axis=0, tiled=True),
    )
    sliced = normed
    query_sum, key_sum, value_sum = tuple(
        (jnp.dot(sliced, piece, preferred_element_type=jnp.float32) for piece in pieces)
    )
    head_count = query_width // QK
    queries = query_sum.astype(jnp.bfloat16).reshape(row_count, head_count, QK)
    keys_local = key_sum.astype(jnp.bfloat16).reshape(row_count, head_count, QK)
    values_local = value_sum.astype(jnp.bfloat16).reshape(row_count, head_count, HV)
    moved_query, moved_keys, moved_values = (
        lax.all_to_all(queries, "pr", split_axis=1, concat_axis=0, tiled=True),
        lax.all_to_all(keys_local, "pr", split_axis=1, concat_axis=0, tiled=True),
        lax.all_to_all(values_local, "pr", split_axis=1, concat_axis=0, tiled=True),
    )
    carried = attention_step(
        moved_query,
        attention_start(moved_query),
        (
            lax.all_gather(moved_keys, "seq", axis=0, tiled=True),
            lax.all_gather(moved_values, "seq", axis=0, tiled=True),
        ),
    )
    attended = lax.all_to_all(
        attention_finish(carried), "pr", split_axis=0, concat_axis=1, tiled=True
    )
    attended_flat = attended.reshape(row_count, head_count * HV)
    head_terms = jnp.dot(
        attended_flat,
        lax.all_gather(wo, "pr", axis=1, tiled=True),
        preferred_element_type=jnp.float32,
    )
    own_share = lax.psum_scatter(
        head_terms.astype(jnp.bfloat16), "tp", scatter_dimension=1, tiled=True
    ).astype(jnp.float32)
    trunk = (hidden_conv.astype(jnp.float32) + own_share).astype(jnp.bfloat16)
    pooled = trunk.astype(jnp.float32).reshape(row_count // POOL, POOL, -1).mean(axis=1)
    partial_embed = jnp.dot(pooled, pair_w.astype(jnp.float32), precision=lax.Precision.HIGHEST)
    embedded = lax.psum(partial_embed, "tp").astype(jnp.bfloat16)
    every_embed = lax.all_gather(embedded, ("seq", "pr"), axis=0, tiled=True)
    pair_rows = pair_in.shape[0]
    pair_cols = pair_in.shape[1]
    pair_width = pair_in.shape[2]
    row_first = lax.axis_index(("seq", "tp")) * pair_rows
    col_first = lax.axis_index("pr") * pair_cols
    row_embed = lax.dynamic_slice_in_dim(every_embed, row_first, pair_rows, 0)[
        :, :pair_width
    ].astype(jnp.float32)
    col_embed = lax.dynamic_slice_in_dim(every_embed, col_first, pair_cols, 0)[
        :, pair_width:
    ].astype(jnp.float32)
    summed = pair_in.astype(jnp.float32) + row_embed[:, None, :] + col_embed[None, :, :]
    pair_normed = (summed * rms_scale(summed) * pair_gain).astype(jnp.bfloat16)
    inner = jax.nn.gelu(
        jnp.dot(pair_normed.reshape(-1, pair_width), pair_w1, preferred_element_type=jnp.float32)
    ).astype(jnp.bfloat16)
    update = jnp.dot(inner, pair_w2, preferred_element_type=jnp.float32).reshape(summed.shape)
    pair_out = (summed + update).astype(jnp.bfloat16)
    return (trunk, pair_out)


def solution(mesh):
    in_specs = (
        P(("grp", "seq", "pr"), "tp"),
        P(None, "pr", "tp"),
        P("tp"),
        P(),
        P("pr", "tp"),
        P("pr", "tp"),
        P("pr", "tp"),
        P("tp", "pr"),
        P("tp", None),
        P(("grp", "seq", "tp"), "pr", None),
        P(),
        P(),
        P(),
    )
    out_specs = (P(("grp", "seq", "pr"), "tp"), P(("grp", "seq", "tp"), "pr", None))
    return jax.shard_map(local, mesh=mesh, in_specs=in_specs, out_specs=out_specs, check_vma=False)
```

profile of v0, /device:TPU:0, one launch (start us, length us, event | category | flops | bytes accessed | tf_op | source)
XLA Modules:
  0.0 160.2 jit_solution(4517351203953663694)
XLA Ops:
  7.2 0.7 all-gather.6.cloned.1.call-update
  8.0 0.7 all-gather.12.cloned.1.call-update
  8.7 0.7 all-gather.10.cloned.1.call-update
  10.1 2.4 %collective-permute-start = (bf16[2,384]{1,0:T(2,128)(2,1)S(1)}, bf16[2,384]{1,0:T(2,128)(2,1)S(1)}, u32[]{:S(2)}, u32[]{:S(2)}) collective-permute-start(bf16[2,384]{1,0:T(2,128)(2,1)S(1)} %get-tuple-element.4), channel_id=1, source_target_pairs={{0,1},{1,4},{4,5},{5,8},{8,9},{9,12},{12,13},{2,3},{3,6},{6,7},{7,... | collective-permute-start | bytes 4616 | tf_op jit(solution)/shard_map/ppermute | solution.py:20
  12.5 1.3 collective-permute-start.1
  13.8 3.9 %collective-permute-done.1 = bf16[2,384]{1,0:T(2,128)(2,1)S(1)} collective-permute-done((bf16[2,384]{1,0:T(2,128)(2,1)S(1)}, bf16[2,384]{1,0:T(2,128)(2,1)S(1)}, u32[]{:S(2)}, u32[]{:S(2)}) %collective-permute-start.1) | collective-permute-done | bytes 1568 | tf_op jit(solution)/shard_map/ppermute | solution.py:21
  17.7 5.4 %all_gather.30 = bf16[132,768]{1,0:T(8,128)(2,1)S(1)} all-gather(bf16[132,384]{1,0:T(8,128)(2,1)S(1)} %pad_maximum_fusion), channel_id=1, replica_groups=mesh['grp'=2,'seq'=4,'tp'=2,'pr'=2] {'tp'}, dimensions={1}, use_global_device_ids=true | all-gather | bytes 304128 | tf_op jit(solution)/shard_map/all_gather | solution.py:83
  23.1 5.4 %all-gather.6.cloned.1.call-done = bf16[5,768,768]{2,1,0:T(8,128)(2,1)} async-done(((bf16[5,384,768]{2,1,0:T(8,128)(2,1)}), bf16[5,768,768]{2,1,0:T(8,128)(2,1)}) %all-gather.6.cloned.1.call-update) | async-done | bytes 5898256 | tf_op jit(solution)/shard_map/all_gather | solution.py:86
  28.5 1.6 fusion.3
  30.1 1.6 convolution_add_fusion.3
  31.7 1.6 convolution_add_fusion.2
  33.3 1.6 convolution_add_fusion.1
  34.9 1.7 %multiply_reduce_fusion.1 = (f32[128]{0:T(128)S(1)}, f32[128,768]{1,0:T(8,128)S(1)}) fusion(f32[128,768]{1,0:T(8,128)S(1)} %convolution_add_fusion.1, bf16[5,768,768]{2,1,0:T(8,128)(2,1)} %all-gather.6.cloned.1.call-done, bf16[132,768]{1,0:T(8,128)(2,1)S(1)} %all_gather.30), kind=kOutput, calls=%fused_computation.42 | convolution fusion | flops 151289728 | bytes 2163200 | tf_op jit(solution)/shard_map/dot_general | solution.py:89
  36.6 4.9 %psum.14 = f32[128,1]{0,1:T(1,128)S(1)} all-reduce(f32[128,1]{0,1:T(1,128)S(1)} %bitcast.89), channel_id=1, replica_groups=mesh['grp'=2,'seq'=4,'tp'=2,'pr'=2] {'tp'}, use_global_device_ids=true, to_apply=%region_1.0 | all-reduce | flops 128 | bytes 1024 | tf_op jit(solution)/shard_map/psum | solution.py:92
  41.8 6.6 %all_gather.32 = bf16[128,1536]{1,0:T(8,128)(2,1)S(1)} all-gather(bf16[128,768]{1,0:T(8,128)(2,1)S(1)} %fusion.20), channel_id=1, replica_groups=mesh['grp'=2,'seq'=4,'tp'=2,'pr'=2] {'tp'}, dimensions={1}, use_global_device_ids=true | all-gather | bytes 589824 | tf_op jit(solution)/shard_map/all_gather | solution.py:97
  48.6 2.0 %fusion.6 = bf16[16,4,8,128]{3,2,1,0:T(8,128)(2,1)S(1)} fusion(bf16[1536,512]{1,0:T(8,128)(2,1)} %all-gather.12.cloned.1.call-done, bf16[128,1536]{1,0:T(8,128)(2,1)S(1)} %all_gather.32, f32[1536]{0:T(1024)S(1)} %copy-done.3, f32[128]{0:T(128)S(1)} %add_rsqrt_fusion.1), kind=kOutput, calls=%fused_computation.22 | convolution fusion | flops 202178560 | bytes 2103808 | tf_op jit(solution)/shard_map/dot_general | solution.py:108
  50.6 3.8 %all_to_all.69 = bf16[128,4,128]{2,0,1:T(8,128)(2,1)S(1)} all-to-all(bf16[128,4,128]{2,0,1:T(8,128)(2,1)S(1)} %bitcast.82), channel_id=1, replica_groups=mesh['grp'=2,'seq'=4,'tp'=2,'pr'=2] {'pr'}, dimensions={1} | all-to-all | bytes 262144 | tf_op jit(solution)/shard_map/all_to_all | solution.py:116
  54.5 1.8 %fusion.5 = bf16[16,4,8,128]{3,2,1,0:T(8,128)(2,1)S(1)} fusion(bf16[1536,512]{1,0:T(8,128)(2,1)} %all-gather.10.cloned.1.call-done, bf16[128,1536]{1,0:T(8,128)(2,1)S(1)} %all_gather.32, f32[1536]{0:T(1024)S(1)} %copy-done.3, f32[128]{0:T(128)S(1)} %add_rsqrt_fusion.1), kind=kOutput, calls=%fused_computation.21 | convolution fusion | flops 202178560 | bytes 2103808 | tf_op jit(solution)/shard_map/dot_general | solution.py:108
  56.3 3.8 %all_to_all.70 = bf16[128,4,128]{2,0,1:T(8,128)(2,1)S(1)} all-to-all(bf16[128,4,128]{2,0,1:T(8,128)(2,1)S(1)} %bitcast.84), channel_id=1, replica_groups=mesh['grp'=2,'seq'=4,'tp'=2,'pr'=2] {'pr'}, dimensions={1} | all-to-all | bytes 262144 | tf_op jit(solution)/shard_map/all_to_all | solution.py:115
  60.2 6.9 %all-gather.8.cloned.1.call-done = bf16[1536,768]{1,0:T(8,128)(2,1)} async-done(((bf16[768,768]{1,0:T(8,128)(2,1)}), bf16[1536,768]{1,0:T(8,128)(2,1)}) %all-gather.8.cloned.1.call-update) | async-done | bytes 2359312 | tf_op jit(solution)/shard_map/all_gather | solution.py:104
  67.1 2.2 %convolution_convert_fusion.1 = bf16[128,768]{1,0:T(8,128)(2,1)S(1)} fusion(bf16[1536,768]{1,0:T(8,128)(2,1)} %all-gather.8.cloned.1.call-done, bf16[128,1536]{1,0:T(8,128)(2,1)S(1)} %all_gather.32, f32[1536]{0:T(1024)S(1)} %copy-done.3, f32[128]{0:T(128)S(1)} %add_rsqrt_fusion.1), kind=kOutput, calls=%fused_computation.18 | convolution fusion | flops 302874624 | bytes 2955776 | tf_op jit(solution)/shard_map/dot_general | solution.py:108
  69.5 3.9 %all_to_all.71 = bf16[128,4,192]{0,2,1:T(8,128)(2,1)S(1)} all-to-all(bf16[128,4,192]{0,2,1:T(8,128)(2,1)S(1)} %bitcast.77), channel_id=1, replica_groups=mesh['grp'=2,'seq'=4,'tp'=2,'pr'=2] {'pr'}, dimensions={1} | all-to-all | bytes 393216 | tf_op jit(solution)/shard_map/all_to_all | solution.py:117
  73.4 16.1 %all_gather.37 = bf16[1024,2,128]{2,0,1:T(8,128)(2,1)S(1)} all-gather(bf16[256,2,128]{2,0,1:T(8,128)(2,1)S(1)} %bitcast.80), channel_id=1, replica_groups=mesh['grp'=2,'seq'=4,'tp'=2,'pr'=2] {'seq'}, dimensions={0}, use_global_device_ids=true | all-gather | bytes 655360 | tf_op jit(solution)/shard_map/all_gather | solution.py:123
  90.6 18.9 %all_gather.34 = bf16[1024,2,192]{0,2,1:T(8,128)(2,1)S(1)} all-gather(bf16[256,2,192]{0,2,1:T(8,128)(2,1)S(1)} %bitcast.79), channel_id=1, replica_groups=mesh['grp'=2,'seq'=4,'tp'=2,'pr'=2] {'seq'}, dimensions={0}, use_global_device_ids=true | all-gather | bytes 983040 | tf_op jit(solution)/shard_map/all_gather | solution.py:124
  109.5 0.6 fusion.4
  110.3 3.9 %all_to_all.72 = bf16[256,2,192]{2,1,0:T(2,128)(2,1)S(1)} all-to-all(bf16[256,2,192]{2,1,0:T(2,128)(2,1)S(1)} %copy.36), channel_id=1, replica_groups=mesh['grp'=2,'seq'=4,'tp'=2,'pr'=2] {'pr'}, dimensions={0} | all-to-all | bytes 393216 | tf_op jit(solution)/shard_map/all_to_all | solution.py:127
  114.5 3.0 %convolution_convert_fusion = bf16[128,1536]{1,0:T(8,128)(2,1)} fusion(bf16[128,768]{0,1:T(8,128)(2,1)S(1)} %bitcast.76, bf16[768,1536]{1,0:T(8,128)(2,1)} %all-gather.14.cloned.1.call-done), kind=kOutput, calls=%fused_computation | convolution fusion | flops 302186496 | bytes 2949120 | tf_op jit(solution)/shard_map/dot_general | solution.py:131
  117.5 13.2 %reduce-scatter.2.cloned.1.call-done = bf16[128,768]{1,0:T(8,128)(2,1)} async-done(((bf16[128,1536]{1,0:T(8,128)(2,1)}), bf16[128,768]{1,0:T(8,128)(2,1)}) %reduce-scatter.2.cloned.1.call-update) | async-done | bytes 196624 | tf_op jit(solution)/shard_map/reduce_scatter | solution.py:136
  130.7 1.9 %convert_reduce_fusion = (f32[8,768]{1,0:T(8,128)S(1)}, bf16[128,768]{1,0:T(8,128)(2,1)}) fusion(bf16[128,768]{1,0:T(8,128)(2,1)} %reduce-scatter.2.cloned.1.call-done, f32[768]{0:T(1024)S(1)} %copy-done.4, f32[128,768]{1,0:T(8,128)S(1)} %get-tuple-element.7, f32[128]{0:T(128)S(1)} %rsqrt_bitcast_fusion), kind=kLoop, calls=%fused_computation.39 | loop fusion | flops 1665024 | bytes 814592 | tf_op jit(solution)/shard_map/reduce_sum | solution.py:140
  132.9 5.0 %psum.15 = bf16[8,256]{1,0:T(8,128)(2,1)S(1)} all-reduce(f32[8,256]{1,0:T(8,128)S(1)} %fusion.39), channel_id=1, replica_groups=mesh['grp'=2,'seq'=4,'tp'=2,'pr'=2] {'tp'}, use_global_device_ids=true, to_apply=%region_7.0 | all-reduce | flops 2048 | bytes 12288 | tf_op jit(solution)/shard_map/psum | solution.py:142
  137.9 14.1 %all_gather.39 = bf16[64,256]{1,0:T(8,128)(2,1)S(1)} all-gather(bf16[8,256]{1,0:T(8,128)(2,1)S(1)} %psum.15), channel_id=1, replica_groups=mesh['grp'=2,'seq'=4,'tp'=2,'pr'=2] {'seq','pr'}, dimensions={0}, use_global_device_ids=true | all-gather | bytes 36864 | tf_op jit(solution)/shard_map/all_gather | solution.py:143
  152.7 0.7 add_convert_fusion.1
  (53 shorter events, 3.8 us)
Async XLA Ops:
  7.2 125.5 %copy-start = (bf16[768,256]{1,0:T(8,128)(2,1)S(1)}, bf16[768,256]{1,0:T(8,128)(2,1)}, u32[]{:S(2)}) copy-start(bf16[768,256]{1,0:T(8,128)(2,1)} %param.21) | copy-start | bytes 1179652
  7.2 21.3 %all-gather.6.cloned.1.call-start = ((), (), s32[]{:S(2)}) async-start(), calls=%async_computation.5 | async-start | bytes 8847360 | tf_op jit(solution)/shard_map/all_gather | solution.py:86
  7.9 2.1 %copy-start.2 = (bf16[128,384]{1,0:T(8,128)(2,1)S(1)}, bf16[128,384]{1,0:T(8,128)(2,1)}, u32[]{:S(2)}) copy-start(bf16[128,384]{1,0:T(8,128)(2,1)} %param.13) | copy-start | bytes 294916
  7.9 40.7 %all-gather.12.cloned.1.call-start = ((), (), s32[]{:S(2)}) async-start(), calls=%async_computation.8 | async-start | bytes 2359296 | tf_op jit(solution)/shard_map/all_gather | solution.py:103
  8.7 45.8 %all-gather.10.cloned.1.call-start = ((), (), s32[]{:S(2)}) async-start(), calls=%async_computation.7 | async-start | bytes 2359296 | tf_op jit(solution)/shard_map/all_gather | solution.py:102
  9.4 57.7 %all-gather.8.cloned.1.call-start = ((), (), s32[]{:S(2)}) async-start(), calls=%async_computation.6 | async-start | bytes 3538944 | tf_op jit(solution)/shard_map/all_gather | solution.py:104
  10.0 104.5 %all-gather.14.cloned.1.call-start = ((), (), s32[]{:S(2)}) async-start(), calls=%async_computation.9 | async-start | bytes 3538944 | tf_op jit(solution)/shard_map/all_gather | solution.py:133
  10.1 3.8 %collective-permute-start = (bf16[2,384]{1,0:T(2,128)(2,1)S(1)}, bf16[2,384]{1,0:T(2,128)(2,1)S(1)}, u32[]{:S(2)}, u32[]{:S(2)}) collective-permute-start(bf16[2,384]{1,0:T(2,128)(2,1)S(1)} %get-tuple-element.4), channel_id=1, source_target_pairs={{0,1},{1,4},{4,5},{5,8},{8,9},{9,12},{12,13},{2,3},{3,6},{6,7},{7,... | collective-permute-start | bytes 4616 | tf_op jit(solution)/shard_map/ppermute | solution.py:20
  12.5 5.2 %collective-permute-start.1 = (bf16[2,384]{1,0:T(2,128)(2,1)S(1)}, bf16[2,384]{1,0:T(2,128)(2,1)S(1)}, u32[]{:S(2)}, u32[]{:S(2)}) collective-permute-start(bf16[2,384]{1,0:T(2,128)(2,1)S(1)} %get-tuple-element.5), channel_id=1, source_target_pairs={{1,0},{4,1},{5,4},{8,5},{9,8},{12,9},{13,12},{3,2},{6,3},{7,6},{10... | collective-permute-start | bytes 4616 | tf_op jit(solution)/shard_map/ppermute | solution.py:21
  13.8 116.9 %reduce-scatter.2.cloned.1.call-start = ((), (), s32[]{:S(2)}) async-start(), calls=%async_computation.10 | async-start | bytes 589824 | tf_op jit(solution)/shard_map/reduce_scatter | solution.py:136
  33.3 8.3 %copy-start.4 = (f32[768]{0:T(1024)S(1)}, f32[768]{0:T(1024)}, u32[]{:S(2)}) copy-start(f32[768]{0:T(1024)} %param.15) | copy-start | bytes 9220
  34.9 13.7 %copy-start.3 = (f32[1536]{0:T(1024)S(1)}, f32[1536]{0:T(1024)}, u32[]{:S(2)}) copy-start(f32[1536]{0:T(1024)} %param.16) | copy-start | bytes 18436
  114.5 37.5 %copy-start.1 = (bf16[8,32,128]{2,1,0:T(8,128)(2,1)S(1)}, bf16[8,32,128]{2,1,0:T(8,128)(2,1)}, u32[]{:S(2)}) copy-start(bf16[8,32,128]{2,1,0:T(8,128)(2,1)} %param.22) | copy-start | bytes 196612
  114.5 37.7 %copy-start.5 = (f32[128]{0:T(128)S(1)}, f32[128]{0:T(128)}, u32[]{:S(2)}) copy-start(f32[128]{0:T(128)} %param.23) | copy-start | bytes 1540
  114.5 37.8 %copy-start.6 = (bf16[256,128]{1,0:T(8,128)(2,1)S(1)}, bf16[256,128]{1,0:T(8,128)(2,1)}, u32[]{:S(2)}) copy-start(bf16[256,128]{1,0:T(8,128)(2,1)} %param.25) | copy-start | bytes 196612
  114.5 37.8 %copy-start.7 = (bf16[128,256]{1,0:T(8,128)(2,1)S(1)}, bf16[128,256]{1,0:T(8,128)(2,1)}, u32[]{:S(2)}) copy-start(bf16[128,256]{1,0:T(8,128)(2,1)} %param.24) | copy-start | bytes 196612
Sparse Core Ops, SparseCore 0:
  9.5 18.8 all-gather.5
  30.0 10.9 all-gather.11
  42.6 10.9 all-gather.9
  55.0 12.1 all-gather.7
  68.5 12.1 all-gather.13
  117.7 13.0 reduce-scatter.1
where the time goes:
time: 161 us; the launch traced here: 160 us
  blocking collectives  86.6 us (54%)
  waiting for transfers between devices  32 us (20%)
  matrix products  18.8 us (12%)
  between operations  14.4 us (9%)
  starting transfers between devices  3.92 us (2%)
  other arithmetic  3.73 us (2%)
    all_gather x1, blocking collectives, local(): lax.all_gather(moved_values, 'seq', axis=0, tiled=True)  18.9 us
    all_gather x1, blocking collectives, local(): lax.all_gather(moved_keys, 'seq', axis=0, tiled=True)  16.1 us
    all_gather x1, blocking collectives, local(): every_embed = lax.all_gather(embedded, ('seq', 'pr'), axis=0, tiled=True)  14.1 us
    reduce_scatter x1, waiting for transfers between devices, local(): lax.psum_scatter(head_terms.astype(jnp.bfloat16), 'tp', scatter_dimension...  13.2 us
    dot_general x5, matrix products, local(): jnp.dot(sliced[offset:offset + row_count], piece[offset], preferred_eleme...  8.08 us
    all_gather x1, waiting for transfers between devices, local(): lax.all_gather(wv, 'pr', axis=0, tiled=True)  6.94 us
    all_gather x1, blocking collectives, local(): trunk_full = lax.all_gather(hidden_conv, 'tp', axis=1, tiled=True)  6.61 us
    dot_general x3, matrix products, local(): jnp.dot(sliced, piece, preferred_element_type=jnp.float32)  5.97 us
  transfers between devices with their start and end apart: 8, of which 4 were waited for; matrix products, arithmetic and copies ran while one was open for 10% of the time, Pallas kernels for 0%

commit v1 on v0

--- a/solution.py
+++ b/solution.py
@@ -8,6 +8,16 @@
 HV = 192
 POOL = 16
 EPSILON = 1e-06
+
+
+def collect(x, axis, dim):
+    ways, here, step = (lax.axis_size(axis), lax.axis_index(axis), x.shape[dim])
+    shape = [n * ways if d == dim else n for d, n in enumerate(x.shape)]
+    full = lax.dynamic_update_slice_in_dim(jnp.zeros(shape, x.dtype), x, here * step, axis=dim)
+    for far in range(1, ways):
+        x = lax.ppermute(x, axis, [(d, (d + 1) % ways) for d in range(ways)])
+        full = lax.dynamic_update_slice_in_dim(full, x, (here - far) % ways * step, axis=dim)
+    return full
 
 
 def extended(value, sides, width):
@@ -119,10 +129,7 @@
     carried = attention_step(
         moved_query,
         attention_start(moved_query),
-        (
-            lax.all_gather(moved_keys, "seq", axis=0, tiled=True),
-            lax.all_gather(moved_values, "seq", axis=0, tiled=True),
-        ),
+        (collect(moved_keys, "seq", 0), lax.all_gather(moved_values, "seq", axis=0, tiled=True)),
     )
     attended = lax.all_to_all(
         attention_finish(carried), "pr", split_axis=0, concat_axis=1, tiled=True

time: 161 us -> 156 us (0.969)
  blocking collectives: 86.6 us -> 66.4 us
  starting transfers between devices: 3.92 us -> 11.2 us
  waiting for transfers between devices: 32 us -> 39.1 us
    all_gather x1 -> x0, blocking collectives: 16.1 us -> none  [local(): lax.all_gather(moved_keys, 'seq', axis=0, tiled=True)]
    all_gather x1, waiting for transfers between devices: 0.02 us -> 8.69 us  [local(): lax.all_gather(wq, 'pr', axis=0, tiled=True)]
    all_gather x1, waiting for transfers between devices: 6.94 us -> 0.01 us  [local(): lax.all_gather(wv, 'pr', axis=0, tiled=True)]
    ppermute x0 -> x3, waiting for transfers between devices: none -> 6.62 us  [collect(): x = lax.ppermute(x, axis, [(d, (d + 1) % ways) for d in range(ways)])]
    ppermute x0 -> x3, starting transfers between devices: none -> 3.89 us  [collect(): x = lax.ppermute(x, axis, [(d, (d + 1) % ways) for d in range(ways)])]
    all_to_all x1 -> x0, blocking collectives: 3.84 us -> none  [local(): lax.all_to_all(queries, 'pr', split_axis=1, concat_axis=0, tiled=True)]
    all_to_all x0 -> x1, starting transfers between devices: none -> 3.39 us  [local(): lax.all_to_all(queries, 'pr', split_axis=1, concat_axis=0, tiled=True)]
  transfers between devices with their start and end apart: 8 -> 12, of which waited for: 4 -> 5; matrix products, arithmetic and copies ran while one was open for 10% -> 11% of each run, Pallas kernels for 0% -> 0%
where the time goes in v1:
time: 156 us; the launch traced here: 155 us
  blocking collectives  66.4 us (43%)
  waiting for transfers between devices  39.1 us (25%)
  matrix products  18.8 us (12%)
  between operations  14.5 us (9%)
  starting transfers between devices  11.2 us (7%)
  other arithmetic  3.73 us (2%)
    all_gather x1, blocking collectives, local(): lax.all_gather(moved_values, 'seq', axis=0, tiled=True)  18.6 us
    all_gather x1, blocking collectives, local(): every_embed = lax.all_gather(embedded, ('seq', 'pr'), axis=0, tiled=True)  14.1 us
    reduce_scatter x1, waiting for transfers between devices, local(): lax.psum_scatter(head_terms.astype(jnp.bfloat16), 'tp', scatter_dimension...  12 us
    all_gather x1, waiting for transfers between devices, local(): lax.all_gather(wq, 'pr', axis=0, tiled=True)  8.69 us
    dot_general x5, matrix products, local(): jnp.dot(sliced[offset:offset + row_count], piece[offset], preferred_eleme...  8.08 us
    ppermute x3, waiting for transfers between devices, collect(): x = lax.ppermute(x, axis, [(d, (d + 1) % ways) for d in range(ways)])  6.62 us
    all_gather x1, blocking collectives, local(): trunk_full = lax.all_gather(hidden_conv, 'tp', axis=1, tiled=True)  6.61 us
    dot_general x3, matrix products, local(): jnp.dot(sliced, piece, preferred_element_type=jnp.float32)  6.01 us
  transfers between devices with their start and end apart: 12, of which 5 were waited for; matrix products, arithmetic and copies ran while one was open for 11% of the time, Pallas kernels for 0%

profile of v1, /device:TPU:0, one launch (start us, length us, event | category | flops | bytes accessed | tf_op | source)
XLA Modules:
  0.0 155.3 jit_solution(12905304796393048935)
XLA Ops:
  7.2 0.7 all-gather.6.cloned.1.call-update
  8.0 0.7 all-gather.12.cloned.1.call-update
  8.7 0.7 all-gather.8.cloned.1.call-update
  10.1 2.4 %collective-permute-start = (bf16[2,384]{1,0:T(2,128)(2,1)S(1)}, bf16[2,384]{1,0:T(2,128)(2,1)S(1)}, u32[]{:S(2)}, u32[]{:S(2)}) collective-permute-start(bf16[2,384]{1,0:T(2,128)(2,1)S(1)} %get-tuple-element.4), channel_id=1, source_target_pairs={{0,1},{1,4},{4,5},{5,8},{8,9},{9,12},{12,13},{2,3},{3,6},{6,7},{7,... | collective-permute-start | bytes 4616 | tf_op jit(solution)/shard_map/ppermute | solution.py:30
  12.5 1.3 collective-permute-start.1
  13.9 3.8 %collective-permute-done.1 = bf16[2,384]{1,0:T(2,128)(2,1)S(1)} collective-permute-done((bf16[2,384]{1,0:T(2,128)(2,1)S(1)}, bf16[2,384]{1,0:T(2,128)(2,1)S(1)}, u32[]{:S(2)}, u32[]{:S(2)}) %collective-permute-start.1) | collective-permute-done | bytes 1568 | tf_op jit(solution)/shard_map/ppermute | solution.py:31
  17.7 5.4 %all_gather.27 = bf16[132,768]{1,0:T(8,128)(2,1)S(1)} all-gather(bf16[132,384]{1,0:T(8,128)(2,1)S(1)} %pad_maximum_fusion), channel_id=1, replica_groups=mesh['grp'=2,'seq'=4,'tp'=2,'pr'=2] {'tp'}, dimensions={1}, use_global_device_ids=true | all-gather | bytes 304128 | tf_op jit(solution)/shard_map/all_gather | solution.py:93
  23.1 5.4 %all-gather.6.cloned.1.call-done = bf16[5,768,768]{2,1,0:T(8,128)(2,1)} async-done(((bf16[5,384,768]{2,1,0:T(8,128)(2,1)}), bf16[5,768,768]{2,1,0:T(8,128)(2,1)}) %all-gather.6.cloned.1.call-update) | async-done | bytes 5898256 | tf_op jit(solution)/shard_map/all_gather | solution.py:96
  28.5 1.6 %fusion.2 = f32[128,768]{1,0:T(8,128)S(1)} fusion(bf16[5,768,768]{2,1,0:T(8,128)(2,1)} %all-gather.6.cloned.1.call-done, bf16[132,768]{1,0:T(8,128)(2,1)S(1)} %all_gather.27), kind=kOutput, calls=%fused_computation.14 | convolution fusion | flops 150994944 | bytes 1769472 | tf_op jit(solution)/shard_map/dot_general | solution.py:99
  30.1 1.6 %convolution_add_fusion.3 = f32[128,768]{1,0:T(8,128)S(1)} fusion(f32[128,768]{1,0:T(8,128)S(1)} %fusion.2, bf16[5,768,768]{2,1,0:T(8,128)(2,1)} %all-gather.6.cloned.1.call-done, bf16[132,768]{1,0:T(8,128)(2,1)S(1)} %all_gather.27), kind=kOutput, calls=%fused_computation.9 | convolution fusion | flops 151093248 | bytes 2162688 | tf_op jit(solution)/shard_map/dot_general | solution.py:99
  31.7 1.6 %convolution_add_fusion.2 = f32[128,768]{1,0:T(8,128)S(1)} fusion(f32[128,768]{1,0:T(8,128)S(1)} %convolution_add_fusion.3, bf16[5,768,768]{2,1,0:T(8,128)(2,1)} %all-gather.6.cloned.1.call-done, bf16[132,768]{1,0:T(8,128)(2,1)S(1)} %all_gather.27), kind=kOutput, calls=%fused_computation.8 | convolution fusion | flops 151093248 | bytes 2162688 | tf_op jit(solution)/shard_map/dot_general | solution.py:99
  33.3 1.6 %convolution_add_fusion.1 = f32[128,768]{1,0:T(8,128)S(1)} fusion(f32[128,768]{1,0:T(8,128)S(1)} %convolution_add_fusion.2, bf16[5,768,768]{2,1,0:T(8,128)(2,1)} %all-gather.6.cloned.1.call-done, bf16[132,768]{1,0:T(8,128)(2,1)S(1)} %all_gather.27), kind=kOutput, calls=%fused_computation.7 | convolution fusion | flops 151093248 | bytes 2162688 | tf_op jit(solution)/shard_map/dot_general | solution.py:99
  34.9 1.7 %multiply_reduce_fusion.1 = (f32[128]{0:T(128)S(1)}, f32[128,768]{1,0:T(8,128)S(1)}) fusion(f32[128,768]{1,0:T(8,128)S(1)} %convolution_add_fusion.1, bf16[5,768,768]{2,1,0:T(8,128)(2,1)} %all-gather.6.cloned.1.call-done, bf16[132,768]{1,0:T(8,128)(2,1)S(1)} %all_gather.27), kind=kOutput, calls=%fused_computation.41 | convolution fusion | flops 151289728 | bytes 2163200 | tf_op jit(solution)/shard_map/dot_general | solution.py:99
  36.6 4.9 %psum.14 = f32[128,1]{0,1:T(1,128)S(1)} all-reduce(f32[128,1]{0,1:T(1,128)S(1)} %bitcast.87), channel_id=1, replica_groups=mesh['grp'=2,'seq'=4,'tp'=2,'pr'=2] {'tp'}, use_global_device_ids=true, to_apply=%region_1.0 | all-reduce | flops 128 | bytes 1024 | tf_op jit(solution)/shard_map/psum | solution.py:102
  41.8 6.6 %all_gather.29 = bf16[128,1536]{1,0:T(8,128)(2,1)S(1)} all-gather(bf16[128,768]{1,0:T(8,128)(2,1)S(1)} %fusion.18), channel_id=1, replica_groups=mesh['grp'=2,'seq'=4,'tp'=2,'pr'=2] {'tp'}, dimensions={1}, use_global_device_ids=true | all-gather | bytes 589824 | tf_op jit(solution)/shard_map/all_gather | solution.py:107
  48.6 2.0 %fusion.4 = bf16[16,4,8,128]{3,2,1,0:T(8,128)(2,1)S(1)} fusion(bf16[1536,512]{1,0:T(8,128)(2,1)} %all-gather.12.cloned.1.call-done, bf16[128,1536]{1,0:T(8,128)(2,1)S(1)} %all_gather.29, f32[1536]{0:T(1024)S(1)} %copy-done.3, f32[128]{0:T(128)S(1)} %add_rsqrt_fusion.1), kind=kOutput, calls=%fused_computation.20 | convolution fusion | flops 202178560 | bytes 2103808 | tf_op jit(solution)/shard_map/dot_general | solution.py:118
  50.6 3.9 %all_to_all.69 = bf16[128,4,128]{2,0,1:T(8,128)(2,1)S(1)} all-to-all(bf16[128,4,128]{2,0,1:T(8,128)(2,1)S(1)} %bitcast.82), channel_id=1, replica_groups=mesh['grp'=2,'seq'=4,'tp'=2,'pr'=2] {'pr'}, dimensions={1} | all-to-all | bytes 262144 | tf_op jit(solution)/shard_map/all_to_all | solution.py:126
  54.6 1.8 %collective-permute-start.2 = (bf16[256,2,128]{2,0,1:T(8,128)(2,1)S(1)}, bf16[256,2,128]{2,0,1:T(8,128)(2,1)S(1)}, u32[]{:S(2)}, u32[]{:S(2)}) collective-permute-start(bf16[256,2,128]{2,0,1:T(8,128)(2,1)S(1)} %bitcast.79), channel_id=1, source_target_pairs={{0,4},{4,8},{8,12},{12,0},{1,5},{5,9},{9,13},{13,1},{2,6},{6,10},{... | collective-permute-start | bytes 393224 | tf_op jit(solution)/shard_map/ppermute | solution.py:18
  56.3 2.2 %convolution_convert_fusion.1 = bf16[128,768]{1,0:T(8,128)(2,1)S(1)} fusion(bf16[1536,768]{1,0:T(8,128)(2,1)} %all-gather.8.cloned.1.call-done, bf16[128,1536]{1,0:T(8,128)(2,1)S(1)} %all_gather.29, f32[1536]{0:T(1024)S(1)} %copy-done.3, f32[128]{0:T(128)S(1)} %add_rsqrt_fusion.1), kind=kOutput, calls=%fused_computation.16 | convolution fusion | flops 302874624 | bytes 2955776 | tf_op jit(solution)/shard_map/dot_general | solution.py:118
  58.5 8.7 %all-gather.10.cloned.1.call-done = bf16[1536,512]{1,0:T(8,128)(2,1)} async-done(((bf16[768,512]{1,0:T(8,128)(2,1)}), bf16[1536,512]{1,0:T(8,128)(2,1)}) %all-gather.10.cloned.1.call-update) | async-done | bytes 1572880 | tf_op jit(solution)/shard_map/all_gather | solution.py:112
  67.2 1.8 %fusion.3 = bf16[16,4,8,128]{3,2,1,0:T(8,128)(2,1)S(1)} fusion(bf16[1536,512]{1,0:T(8,128)(2,1)} %all-gather.10.cloned.1.call-done, bf16[128,1536]{1,0:T(8,128)(2,1)S(1)} %all_gather.29, f32[1536]{0:T(1024)S(1)} %copy-done.3, f32[128]{0:T(128)S(1)} %add_rsqrt_fusion.1), kind=kOutput, calls=%fused_computation.19 | convolution fusion | flops 202178560 | bytes 2103808 | tf_op jit(solution)/shard_map/dot_general | solution.py:118
  69.9 3.9 %all_to_all.70 = bf16[128,4,192]{0,2,1:T(8,128)(2,1)S(1)} all-to-all(bf16[128,4,192]{0,2,1:T(8,128)(2,1)S(1)} %bitcast.76), channel_id=1, replica_groups=mesh['grp'=2,'seq'=4,'tp'=2,'pr'=2] {'pr'}, dimensions={1} | all-to-all | bytes 393216 | tf_op jit(solution)/shard_map/all_to_all | solution.py:127
  73.8 3.4 %all-to-all-start.1 = ((bf16[128,4,128]{2,0,1:T(8,128)(2,1)}), bf16[128,4,128]{2,0,1:T(8,128)(2,1)S(1)}, u32[]{:S(2)}, u32[]{:S(2)}) async-start(bf16[128,4,128]{2,0,1:T(8,128)(2,1)} %bitcast.72), calls=%async_computation.1 | async-start | bytes 262144 | tf_op jit(solution)/shard_map/all_to_all | solution.py:125
  77.3 1.8 %collective-permute-start.3 = (bf16[256,2,128]{2,0,1:T(8,128)(2,1)S(1)}, bf16[256,2,128]{2,0,1:T(8,128)(2,1)S(1)}, u32[]{:S(2)}, u32[]{:S(2)}) collective-permute-start(bf16[256,2,128]{2,0,1:T(8,128)(2,1)S(1)} %collective-permute-done.2), channel_id=1, source_target_pairs={{0,4},{4,8},{8,12},{12,0},{1,5},{5,9},{9,13},{13,1},{2,6},{6,10},{... | collective-permute-start | bytes 393224 | tf_op jit(solution)/shard_map/ppermute | solution.py:18
  79.1 18.6 %all_gather.31 = bf16[1024,2,192]{0,2,1:T(8,128)(2,1)S(1)} all-gather(bf16[256,2,192]{0,2,1:T(8,128)(2,1)S(1)} %bitcast.77), channel_id=1, replica_groups=mesh['grp'=2,'seq'=4,'tp'=2,'pr'=2] {'seq'}, dimensions={0}, use_global_device_ids=true | all-gather | bytes 983040 | tf_op jit(solution)/shard_map/all_gather | solution.py:132
  98.2 6.6 %collective-permute-done.4 = bf16[256,2,128]{2,0,1:T(8,128)(2,1)S(1)} collective-permute-done((bf16[256,2,128]{2,0,1:T(8,128)(2,1)S(1)}, bf16[256,2,128]{2,0,1:T(8,128)(2,1)S(1)}, u32[]{:S(2)}, u32[]{:S(2)}) %collective-permute-start.4) | collective-permute-done | bytes 131104 | tf_op jit(solution)/shard_map/ppermute | solution.py:18
  106.8 3.9 %all_to_all.71 = bf16[256,2,192]{2,1,0:T(2,128)(2,1)S(1)} all-to-all(bf16[256,2,192]{2,1,0:T(2,128)(2,1)S(1)} %copy.36), channel_id=1, replica_groups=mesh['grp'=2,'seq'=4,'tp'=2,'pr'=2] {'pr'}, dimensions={0} | all-to-all | bytes 393216 | tf_op jit(solution)/shard_map/all_to_all | solution.py:134
  111.0 3.0 %convolution_convert_fusion = bf16[128,1536]{1,0:T(8,128)(2,1)} fusion(bf16[128,768]{0,1:T(8,128)(2,1)S(1)} %bitcast.74, bf16[768,1536]{1,0:T(8,128)(2,1)} %all-gather.14.cloned.1.call-done), kind=kOutput, calls=%fused_computation | convolution fusion | flops 302186496 | bytes 2949120 | tf_op jit(solution)/shard_map/dot_general | solution.py:138
  114.0 12.0 %reduce-scatter.2.cloned.1.call-done = bf16[128,768]{1,0:T(8,128)(2,1)} async-done(((bf16[128,1536]{1,0:T(8,128)(2,1)}), bf16[128,768]{1,0:T(8,128)(2,1)}) %reduce-scatter.2.cloned.1.call-update) | async-done | bytes 196624 | tf_op jit(solution)/shard_map/reduce_scatter | solution.py:143
  125.9 1.9 %convert_reduce_fusion = (f32[8,768]{1,0:T(8,128)S(1)}, bf16[128,768]{1,0:T(8,128)(2,1)}) fusion(bf16[128,768]{1,0:T(8,128)(2,1)} %reduce-scatter.2.cloned.1.call-done, f32[768]{0:T(1024)S(1)} %copy-done.4, f32[128,768]{1,0:T(8,128)S(1)} %get-tuple-element.7, f32[128]{0:T(128)S(1)} %rsqrt_bitcast_fusion), kind=kLoop, calls=%fused_computation.37 | loop fusion | flops 1665024 | bytes 814592 | tf_op jit(solution)/shard_map/reduce_sum | solution.py:147
  128.1 5.0 %psum.15 = bf16[8,256]{1,0:T(8,128)(2,1)S(1)} all-reduce(f32[8,256]{1,0:T(8,128)S(1)} %fusion.37), channel_id=1, replica_groups=mesh['grp'=2,'seq'=4,'tp'=2,'pr'=2] {'tp'}, use_global_device_ids=true, to_apply=%region_7.8 | all-reduce | flops 2048 | bytes 12288 | tf_op jit(solution)/shard_map/psum | solution.py:149
  133.1 14.1 %all_gather.35 = bf16[64,256]{1,0:T(8,128)(2,1)S(1)} all-gather(bf16[8,256]{1,0:T(8,128)(2,1)S(1)} %psum.15), channel_id=1, replica_groups=mesh['grp'=2,'seq'=4,'tp'=2,'pr'=2] {'seq','pr'}, dimensions={0}, use_global_device_ids=true | all-gather | bytes 36864 | tf_op jit(solution)/shard_map/all_gather | solution.py:150
  (64 shorter events, 6.3 us)
Async XLA Ops:
  7.2 120.7 %copy-start = (bf16[768,256]{1,0:T(8,128)(2,1)S(1)}, bf16[768,256]{1,0:T(8,128)(2,1)}, u32[]{:S(2)}) copy-start(bf16[768,256]{1,0:T(8,128)(2,1)} %param.21) | copy-start | bytes 1179652
  7.2 21.3 %all-gather.6.cloned.1.call-start = ((), (), s32[]{:S(2)}) async-start(), calls=%async_computation.5 | async-start | bytes 8847360 | tf_op jit(solution)/shard_map/all_gather | solution.py:96
  7.9 2.1 %copy-start.2 = (bf16[128,384]{1,0:T(8,128)(2,1)S(1)}, bf16[128,384]{1,0:T(8,128)(2,1)}, u32[]{:S(2)}) copy-start(bf16[128,384]{1,0:T(8,128)(2,1)} %param.13) | copy-start | bytes 294916
  7.9 40.7 %all-gather.12.cloned.1.call-start = ((), (), s32[]{:S(2)}) async-start(), calls=%async_computation.8 | async-start | bytes 2359296 | tf_op jit(solution)/shard_map/all_gather | solution.py:113
  8.7 47.7 %all-gather.8.cloned.1.call-start = ((), (), s32[]{:S(2)}) async-start(), calls=%async_computation.6 | async-start | bytes 3538944 | tf_op jit(solution)/shard_map/all_gather | solution.py:114
  9.4 57.8 %all-gather.10.cloned.1.call-start = ((), (), s32[]{:S(2)}) async-start(), calls=%async_computation.7 | async-start | bytes 2359296 | tf_op jit(solution)/shard_map/all_gather | solution.py:112
  10.0 100.9 %all-gather.14.cloned.1.call-start = ((), (), s32[]{:S(2)}) async-start(), calls=%async_computation.9 | async-start | bytes 3538944 | tf_op jit(solution)/shard_map/all_gather | solution.py:140
  10.1 3.8 %collective-permute-start = (bf16[2,384]{1,0:T(2,128)(2,1)S(1)}, bf16[2,384]{1,0:T(2,128)(2,1)S(1)}, u32[]{:S(2)}, u32[]{:S(2)}) collective-permute-start(bf16[2,384]{1,0:T(2,128)(2,1)S(1)} %get-tuple-element.4), channel_id=1, source_target_pairs={{0,1},{1,4},{4,5},{5,8},{8,9},{9,12},{12,13},{2,3},{3,6},{6,7},{7,... | collective-permute-start | bytes 4616 | tf_op jit(solution)/shard_map/ppermute | solution.py:30
  12.5 5.2 %collective-permute-start.1 = (bf16[2,384]{1,0:T(2,128)(2,1)S(1)}, bf16[2,384]{1,0:T(2,128)(2,1)S(1)}, u32[]{:S(2)}, u32[]{:S(2)}) collective-permute-start(bf16[2,384]{1,0:T(2,128)(2,1)S(1)} %get-tuple-element.5), channel_id=1, source_target_pairs={{1,0},{4,1},{5,4},{8,5},{9,8},{12,9},{13,12},{3,2},{6,3},{7,6},{10... | collective-permute-start | bytes 4616 | tf_op jit(solution)/shard_map/ppermute | solution.py:31
  33.3 8.3 %copy-start.4 = (f32[768]{0:T(1024)S(1)}, f32[768]{0:T(1024)}, u32[]{:S(2)}) copy-start(f32[768]{0:T(1024)} %param.15) | copy-start | bytes 9220
  34.9 13.7 %copy-start.3 = (f32[1536]{0:T(1024)S(1)}, f32[1536]{0:T(1024)}, u32[]{:S(2)}) copy-start(f32[1536]{0:T(1024)} %param.16) | copy-start | bytes 18436
  54.6 22.7 %collective-permute-start.2 = (bf16[256,2,128]{2,0,1:T(8,128)(2,1)S(1)}, bf16[256,2,128]{2,0,1:T(8,128)(2,1)S(1)}, u32[]{:S(2)}, u32[]{:S(2)}) collective-permute-start(bf16[256,2,128]{2,0,1:T(8,128)(2,1)S(1)} %bitcast.79), channel_id=1, source_target_pairs={{0,4},{4,8},{8,12},{12,0},{1,5},{5,9},{9,13},{13,1},{2,6},{6,10},{... | collective-permute-start | bytes 393224 | tf_op jit(solution)/shard_map/ppermute | solution.py:18
  73.8 23.9 %all-to-all-start.1 = ((bf16[128,4,128]{2,0,1:T(8,128)(2,1)}), bf16[128,4,128]{2,0,1:T(8,128)(2,1)S(1)}, u32[]{:S(2)}, u32[]{:S(2)}) async-start(bf16[128,4,128]{2,0,1:T(8,128)(2,1)} %bitcast.72), calls=%async_computation.1 | async-start | bytes 262144 | tf_op jit(solution)/shard_map/all_to_all | solution.py:125
  77.2 48.7 %reduce-scatter.2.cloned.1.call-start = ((), (), s32[]{:S(2)}) async-start(), calls=%async_computation.10 | async-start | bytes 589824 | tf_op jit(solution)/shard_map/reduce_scatter | solution.py:143
  77.3 20.5 %collective-permute-start.3 = (bf16[256,2,128]{2,0,1:T(8,128)(2,1)S(1)}, bf16[256,2,128]{2,0,1:T(8,128)(2,1)S(1)}, u32[]{:S(2)}, u32[]{:S(2)}) collective-permute-start(bf16[256,2,128]{2,0,1:T(8,128)(2,1)S(1)} %collective-permute-done.2), channel_id=1, source_target_pairs={{0,4},{4,8},{8,12},{12,0},{1,5},{5,9},{9,13},{13,1},{2,6},{6,10},{... | collective-permute-start | bytes 393224 | tf_op jit(solution)/shard_map/ppermute | solution.py:18
  97.8 7.0 %collective-permute-start.4 = (bf16[256,2,128]{2,0,1:T(8,128)(2,1)S(1)}, bf16[256,2,128]{2,0,1:T(8,128)(2,1)S(1)}, u32[]{:S(2)}, u32[]{:S(2)}) collective-permute-start(bf16[256,2,128]{2,0,1:T(8,128)(2,1)S(1)} %collective-permute-done.3), channel_id=1, source_target_pairs={{0,4},{4,8},{8,12},{12,0},{1,5},{5,9},{9,13},{13,1},{2,6},{6,10},{... | collective-permute-start | bytes 393224 | tf_op jit(solution)/shard_map/ppermute | solution.py:18
  110.9 36.3 %copy-start.1 = (bf16[8,32,128]{2,1,0:T(8,128)(2,1)S(1)}, bf16[8,32,128]{2,1,0:T(8,128)(2,1)}, u32[]{:S(2)}) copy-start(bf16[8,32,128]{2,1,0:T(8,128)(2,1)} %param.22) | copy-start | bytes 196612
  110.9 36.4 %copy-start.5 = (f32[128]{0:T(128)S(1)}, f32[128]{0:T(128)}, u32[]{:S(2)}) copy-start(f32[128]{0:T(128)} %param.23) | copy-start | bytes 1540
  111.0 36.5 %copy-start.6 = (bf16[256,128]{1,0:T(8,128)(2,1)S(1)}, bf16[256,128]{1,0:T(8,128)(2,1)}, u32[]{:S(2)}) copy-start(bf16[256,128]{1,0:T(8,128)(2,1)} %param.25) | copy-start | bytes 196612
  111.0 36.5 %copy-start.7 = (bf16[128,256]{1,0:T(8,128)(2,1)S(1)}, bf16[128,256]{1,0:T(8,128)(2,1)}, u32[]{:S(2)}) copy-start(bf16[128,256]{1,0:T(8,128)(2,1)} %param.24) | copy-start | bytes 196612
Sparse Core Ops, SparseCore 0:
  9.5 18.8 all-gather.5
  30.0 10.9 all-gather.11
  42.6 12.2 all-gather.7
  56.2 10.9 all-gather.9
  68.6 12.1 all-gather.13
  114.1 11.7 reduce-scatter.1
